TPU v7x, 32 devices: a whole 2x2x4 slice. The times are simulated.
32 devices in a mesh: rows: 4 (over y, x), cols: 8 (over z, core).
Axes of the slice: x: 2, y: 2, z: 4, core: 2. Of those that a mesh axis runs over, the one named last changes fastest.
Arguments:
- right_side: float32 [8192, 2048], P('rows', 'cols'), may hold values from -6 to 6
- inverse_blocks: float32 [8, 1024, 1024], P('rows', 'cols'), may hold values from -2 to 2, as said below
- coupling_blocks: float32 [8, 1024, 1024], P('rows', 'cols'), may hold values from -0.109375 to 0.109375
- prior_solution: float32 [1024, 2048], P(None, 'cols'), may hold values from -6 to 6
Outputs:
- solution: float32 [8192, 2048], P('rows', 'cols')
Inputs may be any that keep to these rules, and one draw needn't show every extreme that they name: inverse_blocks holds the inverses of well conditioned diagonal blocks of the factor.
All inputs are finite; a program needn't handle non-finite values.
Results may differ from a plain program's by a relative error of at most 0.00013.
Values sent between devices are 32-bit elements; how exact they have to be, the bound alone decides.
No kernel may reach another device: no remote copies, remote signals or barrier semaphores. Data moves between devices by JAX's collectives and lax.ppermute only.
A program may use at most 128 MiB of HBM per device.

v0:
```python
import jax
import jax.numpy as jnp
from jax import lax
from jax.sharding import PartitionSpec as P

HIGHEST_PRECISION = lax.Precision.HIGHEST


def shifted(shard, axis, by):
    devices = lax.axis_size(axis)
    pairs = [(i, i + by) for i in range(devices) if 0 <= i + by < devices]
    return lax.ppermute(shard, axis, pairs)


def local(right_side, inverse_blocks, coupling_blocks, prior_solution):
    count_blocks = inverse_blocks.shape[0]
    block_rows = inverse_blocks.shape[2]
    col_width = right_side.shape[1]
    group_count = lax.axis_size("rows")
    row_group = lax.axis_index("rows")
    blocks = right_side.reshape(count_blocks, block_rows, col_width)
    inverse_full, coupling_full = (
        lax.all_gather(inverse_blocks, "cols", axis=1, tiled=True),
        lax.all_gather(coupling_blocks, "cols", axis=1, tiled=True),
    )
    pieces = 1
    wave_cols = col_width // pieces
    solution = jnp.zeros((count_blocks, block_rows, col_width), jnp.float32)
    incoming = jnp.zeros((block_rows, wave_cols), jnp.float32)
    step_count = group_count + pieces - 1
    for step_index in range(step_count):
        wave_index = step_index - row_group
        active = jnp.logical_and(wave_index >= 0, wave_index < pieces)
        previous = jnp.where(row_group == 0, prior_solution, incoming)
        results = []
        for block_index in range(count_blocks):
            local_rhs = blocks[block_index]
            pushed = local_rhs - jnp.dot(
                coupling_full[block_index],
                previous,
                precision=HIGHEST_PRECISION,
                preferred_element_type=jnp.float32,
            )
            previous = jnp.dot(
                inverse_full[block_index],
                pushed,
                precision=HIGHEST_PRECISION,
                preferred_element_type=jnp.float32,
            )
            results.append(previous)
        stacked = jnp.stack(results)
        current = solution
        solution = jnp.where(active, stacked, current)
        if step_index + 1 < step_count:
            incoming = shifted(previous, "rows", 1)
    return solution.reshape(count_blocks * block_rows, col_width)


def solution(mesh):
    placed = (P("rows", "cols"), P("rows", "cols", None), P("rows", "cols", None), P(None, "cols"))
    return jax.shard_map(
        local, mesh=mesh, in_specs=placed, out_specs=P("rows", "cols"), check_vma=False
    )
```

profile of v0, /device:TPU:4, one launch (start us, length us, event | category | flops | bytes accessed | tf_op | source)
XLA Modules:
  0.0 361.7 jit_solution(14020077271531396193)
XLA Ops:
  6.5 0.0 all-gather.3.cloned.1.call-start
  6.5 0.7 all-gather.3.cloned.1.call-update
  7.3 0.0 all-gather.5.cloned.1.call-start
  7.3 0.7 all-gather.5.cloned.1.call-update
  8.0 1.6 copy.12
  9.6 82.6 %all-gather.3.cloned.1.call-done = f32[2,1024,1024]{2,1,0:T(8,128)} async-done(((f32[2,128,1024]{2,1,0:T(8,128)}), f32[2,1024,1024]{2,1,0:T(8,128)}) %all-gather.3.cloned.1.call-update) | async-done | bytes 8388624 | tf_op jit(solution)/shard_map/all_gather | solution.py:24
  92.2 0.0 copy-done.1
  92.2 6.6 %fusion.26 = f32[1024,256]{1,0:T(8,128)} fusion(f32[2,1024,1024]{2,1,0:T(8,128)} %all-gather.3.cloned.1.call-done, f32[1024,256]{0,1:T(8,128)S(1)} %copy.12, f32[2048,256]{1,0:T(8,128)S(1)} %copy-done.1, pred[]{:T(512)S(6)} %eq.2), kind=kOutput, calls=%fused_computation.34 | convolution fusion | flops 3221749760 | bytes 7340033 | tf_op jit(solution)/shard_map/dot_general | solution.py:38
  98.8 75.5 %all-gather.5.cloned.1.call-done = f32[2,1024,1024]{2,1,0:T(8,128)} async-done(((f32[2,128,1024]{2,1,0:T(8,128)}), f32[2,1024,1024]{2,1,0:T(8,128)}) %all-gather.5.cloned.1.call-update) | async-done | bytes 8388624 | tf_op jit(solution)/shard_map/all_gather | solution.py:23
  174.4 9.1 %fusion.7 = f32[256,1024]{1,0:T(8,128)S(1)} fusion(f32[1024,256]{1,0:T(8,128)} %fusion.26, f32[2,1024,1024]{2,1,0:T(8,128)} %all-gather.5.cloned.1.call-done), kind=kOutput, calls=%fused_computation.11 | convolution fusion | flops 3221225472 | bytes 6291456 | tf_op jit(solution)/shard_map/dot_general | solution.py:44
  183.5 0.0 copy-start.2
  183.5 0.0 slice-start.1
  183.5 6.3 %fusion.18 = f32[1024,256]{1,0:T(8,128)S(1)} fusion(f32[256,1024]{1,0:T(8,128)S(1)} %fusion.7, f32[2,1024,1024]{2,1,0:T(8,128)} %all-gather.3.cloned.1.call-done, f32[2048,256]{1,0:T(8,128)S(1)} %copy-done.1), kind=kOutput, calls=%fused_computation.26 | convolution fusion | flops 3221487616 | bytes 7340032 | tf_op jit(solution)/shard_map/dot_general | solution.py:38
  189.9 0.0 copy-done
  189.9 7.1 %fusion.15 = f32[256,1024]{1,0:T(8,128)S(1)} fusion(f32[1024,256]{1,0:T(8,128)S(1)} %fusion.18, f32[2,1024,1024]{2,1,0:T(8,128)S(1)} %copy-done), kind=kOutput, calls=%fused_computation.19 | convolution fusion | flops 3221225472 | bytes 6291456 | tf_op jit(solution)/shard_map/dot_general | solution.py:44
  196.9 0.0 copy-done.2
  196.9 0.0 copy-start.8
  196.9 3.5 collective-permute-start
  200.5 24.5 %collective-permute-done = f32[1024,256]{0,1:T(8,128)S(1)} collective-permute-done((f32[1024,256]{0,1:T(8,128)S(1)}, f32[1024,256]{0,1:T(8,128)S(1)}, u32[]{:S(2)}, u32[]{:S(2)}) %collective-permute-start) | collective-permute-done | bytes 1048608 | tf_op jit(solution)/shard_map/ppermute | solution.py:12
  225.0 0.0 slice-done
  225.0 0.0 slice-done.1
  225.0 3.5 fusion.28
  228.5 0.0 copy-done.8
  228.6 7.1 %fusion.6 = f32[256,1024]{1,0:T(8,128)S(1)} fusion(f32[1024,256]{1,0:T(8,128)S(1)} %fusion.28, f32[2,1024,1024]{2,1,0:T(8,128)S(1)} %copy-done), kind=kOutput, calls=%fused_computation.10 | convolution fusion | flops 3221225472 | bytes 6291456 | tf_op jit(solution)/shard_map/dot_general | solution.py:44
  235.6 0.0 copy-start.4
  235.6 3.7 %fusion.20 = f32[1024,256]{1,0:T(8,128)S(1)} fusion(f32[256,1024]{1,0:T(8,128)S(1)} %fusion.6, f32[2,1024,1024]{2,1,0:T(8,128)S(1)} %bitcast.129, f32[2048,256]{1,0:T(8,128)S(1)} %copy-done.1), kind=kOutput, calls=%fused_computation.28 | convolution fusion | flops 3221487616 | bytes 7340032 | tf_op jit(solution)/shard_map/dot_general | solution.py:38
  239.4 7.1 %fusion.14 = f32[256,1024]{1,0:T(8,128)S(1)} fusion(f32[1024,256]{1,0:T(8,128)S(1)} %fusion.20, f32[2,1024,1024]{2,1,0:T(8,128)S(1)} %copy-done), kind=kOutput, calls=%fused_computation.18 | convolution fusion | flops 3221225472 | bytes 6291456 | tf_op jit(solution)/shard_map/dot_general | solution.py:44
  246.4 0.0 copy-done.4
  246.4 0.0 copy-start.10
  246.4 2.9 collective-permute-start.1
  249.3 24.3 %collective-permute-done.1 = f32[1024,256]{0,1:T(8,128)S(1)} collective-permute-done((f32[1024,256]{0,1:T(8,128)S(1)}, f32[1024,256]{0,1:T(8,128)S(1)}, u32[]{:S(2)}, u32[]{:S(2)}) %collective-permute-start.1) | collective-permute-done | bytes 1048608 | tf_op jit(solution)/shard_map/ppermute | solution.py:12
  273.7 3.5 fusion.30
  277.2 0.0 copy-done.10
  277.2 7.1 %fusion.5 = f32[256,1024]{1,0:T(8,128)S(1)} fusion(f32[1024,256]{1,0:T(8,128)S(1)} %fusion.30, f32[2,1024,1024]{2,1,0:T(8,128)S(1)} %copy-done), kind=kOutput, calls=%fused_computation.9 | convolution fusion | flops 3221225472 | bytes 6291456 | tf_op jit(solution)/shard_map/dot_general | solution.py:44
  284.3 0.0 copy-start.6
  284.3 3.7 %fusion.22 = f32[1024,256]{1,0:T(8,128)S(1)} fusion(f32[256,1024]{1,0:T(8,128)S(1)} %fusion.5, f32[2,1024,1024]{2,1,0:T(8,128)S(1)} %bitcast.129, f32[2048,256]{1,0:T(8,128)S(1)} %copy-done.1), kind=kOutput, calls=%fused_computation.30 | convolution fusion | flops 3221487616 | bytes 7340032 | tf_op jit(solution)/shard_map/dot_general | solution.py:38
  287.9 8.0 %fusion.13 = f32[256,1024]{1,0:T(8,128)} fusion(f32[1024,256]{1,0:T(8,128)S(1)} %fusion.22, f32[2,1024,1024]{2,1,0:T(8,128)S(1)} %copy-done), kind=kOutput, calls=%fused_computation.17 | convolution fusion | flops 3221225472 | bytes 6291456 | tf_op jit(solution)/shard_map/dot_general | solution.py:44
  296.0 0.0 copy-done.6
  296.0 2.1 collective-permute-start.2
  298.1 24.5 %collective-permute-done.2 = f32[1024,256]{0,1:T(8,128)} collective-permute-done((f32[1024,256]{0,1:T(8,128)}, f32[1024,256]{0,1:T(8,128)}, u32[]{:S(2)}, u32[]{:S(2)}) %collective-permute-start.2) | collective-permute-done | bytes 1048608 | tf_op jit(solution)/shard_map/ppermute | solution.py:12
  322.7 5.8 %fusion.32 = f32[1024,256]{1,0:T(8,128)S(1)} fusion(f32[2,1024,1024]{2,1,0:T(8,128)} %all-gather.3.cloned.1.call-done, f32[1024,256]{0,1:T(8,128)S(1)} %copy.12, f32[1024,256]{0,1:T(8,128)} %collective-permute-done.2, f32[2048,256]{1,0:T(8,128)S(1)} %copy-done.1, pred[]{:T(512)S(6)} %eq.2), kind=kOutput, calls=%fused_computation.40 | convolution fusion | flops 3221749760 | bytes 8388609 | tf_op jit(solution)/shard_map/dot_general | solution.py:38
  328.4 0.0 slice-start.3
  328.4 9.4 %fusion.4 = f32[256,1024]{1,0:T(8,128)S(1)} fusion(f32[1024,256]{1,0:T(8,128)S(1)} %fusion.32, f32[2,1024,1024]{2,1,0:T(8,128)} %all-gather.5.cloned.1.call-done), kind=kOutput, calls=%fused_computation.8 | convolution fusion | flops 3221225472 | bytes 6291456 | tf_op jit(solution)/shard_map/dot_general | solution.py:44
  337.8 5.6 %fusion.24 = f32[1024,256]{1,0:T(8,128)S(1)} fusion(f32[256,1024]{1,0:T(8,128)S(1)} %fusion.4, f32[2,1024,1024]{2,1,0:T(8,128)} %all-gather.3.cloned.1.call-done, f32[2048,256]{1,0:T(8,128)S(1)} %copy-done.1), kind=kOutput, calls=%fused_computation.32 | convolution fusion | flops 3221487616 | bytes 7340032 | tf_op jit(solution)/shard_map/dot_general | solution.py:38
  343.4 0.0 slice-done.2
  343.5 7.1 %fusion.16 = f32[1,1024,256]{1,2,0:T(8,128)S(1)} fusion(f32[1024,256]{1,0:T(8,128)S(1)} %fusion.24, f32[2,1024,1024]{2,1,0:T(8,128)S(1)} %bitcast.131), kind=kOutput, calls=%fused_computation.24 | convolution fusion | flops 3221225472 | bytes 6291456 | tf_op jit(solution)/shard_map/dot_general | solution.py:44
  350.6 2.2 maximum_select_fusion
  352.8 1.8 copy.13
  (17 shorter events, 0.0 us)
Async XLA Ops:
  6.5 85.7 %copy-start.1 = (f32[2048,256]{1,0:T(8,128)S(1)}, f32[2048,256]{1,0:T(8,128)}, u32[]{:S(2)}) copy-start(f32[2048,256]{1,0:T(8,128)} %param.4) | copy-start | bytes 6291460
  6.5 85.7 %all-gather.3.cloned.1.call-start = ((), (), s32[]{:S(2)}) async-start(), calls=%async_computation | async-start | bytes 9437184 | tf_op jit(solution)/shard_map/all_gather | solution.py:24
  7.3 167.1 %all-gather.5.cloned.1.call-start = ((), (), s32[]{:S(2)}) async-start(), calls=%async_computation.1 | async-start | bytes 9437184 | tf_op jit(solution)/shard_map/all_gather | solution.py:23
  174.4 15.5 %copy-start = (f32[2,1024,1024]{2,1,0:T(8,128)S(1)}, f32[2,1024,1024]{2,1,0:T(8,128)}, u32[]{:S(2)}) copy-start(f32[2,1024,1024]{2,1,0:T(8,128)} %all-gather.5.cloned.1.call-done) | copy-start | bytes 25165828
  174.4 50.7 %slice-start = ((s8[8388608]{0:T(1024)(128)(4,1)}), s8[4194304]{0:T(1024)(128)(4,1)S(1)}, s32[]{:S(2)}) async-start(s8[8388608]{0:T(1024)(128)(4,1)} %bitcast.128), calls=%async_computation.2 | async-start | bytes 8388608
  183.5 13.4 %copy-start.2 = (f32[256,1024]{1,0:T(8,128)}, f32[256,1024]{1,0:T(8,128)S(1)}, u32[]{:S(2)}) copy-start(f32[256,1024]{1,0:T(8,128)S(1)} %fusion.7) | copy-start | bytes 3145732
  183.5 41.5 %slice-start.1 = ((s8[8388608]{0:T(1024)(128)(4,1)}), s8[4194304]{0:T(1024)(128)(4,1)S(1)}, s32[]{:S(2)}) async-start(s8[8388608]{0:T(1024)(128)(4,1)} %bitcast.128), calls=%async_computation.3 | async-start | bytes 8388608
  196.9 31.6 %copy-start.8 = (f32[256,1024]{1,0:T(8,128)}, f32[256,1024]{1,0:T(8,128)S(1)}, u32[]{:S(2)}) copy-start(f32[256,1024]{1,0:T(8,128)S(1)} %fusion.15) | copy-start | bytes 3145732
  196.9 28.1 %collective-permute-start = (f32[1024,256]{0,1:T(8,128)S(1)}, f32[1024,256]{0,1:T(8,128)S(1)}, u32[]{:S(2)}, u32[]{:S(2)}) collective-permute-start(f32[1024,256]{0,1:T(8,128)S(1)} %bitcast.136), channel_id=1, source_target_pairs={{0,8},{8,16},{16,24},{1,9},{9,17},{17,25},{2,10},{10,18},{18,26},{... | collective-permute-start | bytes 3145736 | tf_op jit(solution)/shard_map/ppermute | solution.py:12
  235.6 10.8 %copy-start.4 = (f32[256,1024]{1,0:T(8,128)}, f32[256,1024]{1,0:T(8,128)S(1)}, u32[]{:S(2)}) copy-start(f32[256,1024]{1,0:T(8,128)S(1)} %fusion.6) | copy-start | bytes 3145732
  246.4 30.7 %copy-start.10 = (f32[256,1024]{1,0:T(8,128)}, f32[256,1024]{1,0:T(8,128)S(1)}, u32[]{:S(2)}) copy-start(f32[256,1024]{1,0:T(8,128)S(1)} %fusion.14) | copy-start | bytes 3145732
  246.4 27.2 %collective-permute-start.1 = (f32[1024,256]{0,1:T(8,128)S(1)}, f32[1024,256]{0,1:T(8,128)S(1)}, u32[]{:S(2)}, u32[]{:S(2)}) collective-permute-start(f32[1024,256]{0,1:T(8,128)S(1)} %bitcast.138), channel_id=1, source_target_pairs={{0,8},{8,16},{16,24},{1,9},{9,17},{17,25},{2,10},{10,18},{18,26},{... | collective-permute-start | bytes 3145736 | tf_op jit(solution)/shard_map/ppermute | solution.py:12
  284.3 11.7 %copy-start.6 = (f32[256,1024]{1,0:T(8,128)}, f32[256,1024]{1,0:T(8,128)S(1)}, u32[]{:S(2)}) copy-start(f32[256,1024]{1,0:T(8,128)S(1)} %fusion.5) | copy-start | bytes 3145732
  296.0 26.7 %collective-permute-start.2 = (f32[1024,256]{0,1:T(8,128)}, f32[1024,256]{0,1:T(8,128)}, u32[]{:S(2)}, u32[]{:S(2)}) collective-permute-start(f32[1024,256]{0,1:T(8,128)} %bitcast.12), channel_id=1, source_target_pairs={{0,8},{8,16},{16,24},{1,9},{9,17},{17,25},{2,10},{10,18},{18,26},{... | collective-permute-start | bytes 3145736 | tf_op jit(solution)/shard_map/ppermute | solution.py:12
  322.7 20.7 %slice-start.2 = ((s8[8388608]{0:T(1024)(128)(4,1)}), s8[4194304]{0:T(1024)(128)(4,1)S(1)}, s32[]{:S(2)}) async-start(s8[8388608]{0:T(1024)(128)(4,1)} %bitcast.130), calls=%async_computation.4 | async-start | bytes 8388608
  328.4 15.0 %slice-start.3 = ((s8[8388608]{0:T(1024)(128)(4,1)}), s8[4194304]{0:T(1024)(128)(4,1)S(1)}, s32[]{:S(2)}) async-start(s8[8388608]{0:T(1024)(128)(4,1)} %bitcast.130), calls=%async_computation.5 | async-start | bytes 8388608
  343.4 7.1 %copy-start.3 = (f32[256,1024]{1,0:T(8,128)S(1)}, f32[256,1024]{1,0:T(8,128)}, u32[]{:S(2)}) copy-start(f32[256,1024]{1,0:T(8,128)} %copy-done.2) | copy-start | bytes 3145732
  343.4 7.1 %copy-start.5 = (f32[256,1024]{1,0:T(8,128)S(1)}, f32[256,1024]{1,0:T(8,128)}, u32[]{:S(2)}) copy-start(f32[256,1024]{1,0:T(8,128)} %copy-done.4) | copy-start | bytes 3145732
  343.4 7.1 %copy-start.7 = (f32[256,1024]{1,0:T(8,128)S(1)}, f32[256,1024]{1,0:T(8,128)}, u32[]{:S(2)}) copy-start(f32[256,1024]{1,0:T(8,128)} %copy-done.6) | copy-start | bytes 3145732
  343.4 7.1 %copy-start.9 = (f32[256,1024]{1,0:T(8,128)S(1)}, f32[256,1024]{1,0:T(8,128)}, u32[]{:S(2)}) copy-start(f32[256,1024]{1,0:T(8,128)} %copy-done.8) | copy-start | bytes 3145732
  343.5 7.1 %copy-start.11 = (f32[256,1024]{1,0:T(8,128)S(1)}, f32[256,1024]{1,0:T(8,128)}, u32[]{:S(2)}) copy-start(f32[256,1024]{1,0:T(8,128)} %copy-done.10) | copy-start | bytes 3145732
Sparse Core Ops, SparseCore 0:
  8.9 83.2 all-gather.2
  93.8 80.5 all-gather.4
where the time goes:
time: 369 us; the launch traced here: 362 us
  waiting for transfers between devices  233 us (63%)
  matrix products  100 us (27%)
  between operations  14 us (4%)
  starting transfers between devices  8.59 us (2%)
    all_gather x1, waiting for transfers between devices, local(): lax.all_gather(coupling_blocks, 'cols', axis=1, tiled=True)  82.6 us
    all_gather x1, waiting for transfers between devices, local(): lax.all_gather(inverse_blocks, 'cols', axis=1, tiled=True)  75.5 us
    ppermute x3, waiting for transfers between devices, shifted(): return lax.ppermute(shard, axis, pairs)  73.4 us
    dot_general x8, matrix products, local(): jnp.dot(inverse_full[block_index], pushed, precision=HIGHEST_PRECISION, p...  61.8 us
    dot_general x8, matrix products, local(): jnp.dot(coupling_full[block_index], previous, precision=HIGHEST_PRECISION...  38.6 us
    ppermute x3, starting transfers between devices, shifted(): return lax.ppermute(shard, axis, pairs)  8.55 us
  transfers between devices with their start and end apart: 5, of which 5 were waited for; matrix products, arithmetic and copies ran while one was open for 2% of the time, Pallas kernels for 0%

commit v1 on v0

--- a/solution.py
+++ b/solution.py
@@ -4,6 +4,12 @@
 from jax.sharding import PartitionSpec as P
 
 HIGHEST_PRECISION = lax.Precision.HIGHEST
+
+
+def gather_by_exchange(x, axis, dim):
+    size = lax.axis_size(axis)
+    repeats = [size if d == dim else 1 for d in range(x.ndim)]
+    return lax.all_to_all(jnp.tile(x, repeats), axis, split_axis=dim, concat_axis=dim, tiled=True)
 
 
 def shifted(shard, axis, by):
@@ -21,7 +27,7 @@
     blocks = right_side.reshape(count_blocks, block_rows, col_width)
     inverse_full, coupling_full = (
         lax.all_gather(inverse_blocks, "cols", axis=1, tiled=True),
-        lax.all_gather(coupling_blocks, "cols", axis=1, tiled=True),
+        gather_by_exchange(coupling_blocks, "cols", 1),
     )
     pieces = 1
     wave_cols = col_width // pieces

time: 369 us -> 456 us (1.24)
  waiting for transfers between devices: 233 us -> 318 us
  local copies, waits for them, and re-layouts: 3.44 us -> 27.7 us
  matrix products: 100 us -> 76.7 us
  starting transfers between devices: 8.59 us -> 13.2 us
    all_to_all x0 -> x1, waiting for transfers between devices: none -> 246 us  [gather_by_exchange(): lax.all_to_all(jnp.tile(x, repeats), axis, split_axis=dim, concat_axis=di...]
    all_gather x1 -> x0, waiting for transfers between devices: 82.6 us -> none  [local(): lax.all_gather(coupling_blocks, 'cols', axis=1, tiled=True)]
    all_gather x1, waiting for transfers between devices: 75.5 us -> 0.01 us  [local(): lax.all_gather(inverse_blocks, 'cols', axis=1, tiled=True)]
    dot_general x8, matrix products: 61.8 us -> 36 us  [local(): jnp.dot(inverse_full[block_index], pushed, precision=HIGHEST_PRECISION, p...]
    slice x0 -> x2, local copies, waits for them, and re-layouts: none -> 12.2 us  [the longest x1 11.1 us: local(): coupling_full[block_index]]
    another operation x0 -> x1, local copies, waits for them, and re-layouts: none -> 6.15 us  [gather_by_exchange(): jnp.tile(x, repeats)]
    unnamed x33 -> x40, local copies, waits for them, and re-layouts: 1.62 us -> 7.53 us
    all_to_all x0 -> x1, starting transfers between devices: none -> 5.15 us  [gather_by_exchange(): lax.all_to_all(jnp.tile(x, repeats), axis, split_axis=dim, concat_axis=di...]
  transfers between devices with their start and end apart: 5 -> 5, of which waited for: 5 -> 4; matrix products, arithmetic and copies ran while one was open for 2% -> 5% of each run, Pallas kernels for 0% -> 0%
where the time goes in v1:
time: 456 us; the launch traced here: 453 us
  waiting for transfers between devices  318 us (70%)
  matrix products  76.7 us (17%)
  local copies, waits for them, and re-layouts  27.7 us (6%)
  between operations  14.3 us (3%)
  starting transfers between devices  13.2 us (3%)
    all_to_all x1, waiting for transfers between devices, gather_by_exchange(): lax.all_to_all(jnp.tile(x, repeats), axis, split_axis=dim, concat_axis=di...  246 us
    ppermute x3, waiting for transfers between devices, shifted(): return lax.ppermute(shard, axis, pairs)  72.1 us
    dot_general x8, matrix products, local(): jnp.dot(coupling_full[block_index], previous, precision=HIGHEST_PRECISION...  40.7 us
    dot_general x8, matrix products, local(): jnp.dot(inverse_full[block_index], pushed, precision=HIGHEST_PRECISION, p...  36 us
    slice x1, local copies, waits for them, and re-layouts, local(): coupling_full[block_index]  11.1 us
  transfers between devices with their start and end apart: 5, of which 4 were waited for; matrix products, arithmetic and copies ran while one was open for 5% of the time, Pallas kernels for 0%

profile of v1, /device:TPU:4, one launch (start us, length us, event | category | flops | bytes accessed | tf_op | source)
XLA Modules:
  0.0 452.5 jit_solution(14295156681972195569)
XLA Ops:
  6.5 2.0 copy.17
  8.6 6.2 %tile.4 = f32[2,8,128,1024]{3,0,2,1:T(2,128)} broadcast(f32[2,128,1024]{2,0,1:T(2,128)S(1)} %copy.17), dimensions={0,2,3} | broadcast | bytes 9437184 | tf_op jit(solution)/shard_map/tile | solution.py:12
  14.7 5.2 %all-to-all-start = ((f32[2,1024,1024]{2,0,1:T(2,128)}), f32[2,1024,1024]{2,0,1:T(2,128)}, u32[]{:S(2)}, u32[]{:S(2)}) async-start(f32[2,1024,1024]{2,0,1:T(2,128)} %bitcast.137), calls=%async_computation | async-start | bytes 16777216 | tf_op jit(solution)/shard_map/all_to_all | solution.py:12
  19.9 0.3 all-gather.2.cloned.1.call-start
  20.2 0.5 all-gather.2.cloned.1.call-update
  20.6 0.0 copy-done.15
  20.6 1.1 fusion.92
  21.7 0.3 copy.24
  22.1 1.6 copy.20
  23.6 1.6 copy.25
  25.2 245.9 %all-to-all-done = f32[2,1024,1024]{2,0,1:T(2,128)} async-done(((f32[2,1024,1024]{2,0,1:T(2,128)}), f32[2,1024,1024]{2,0,1:T(2,128)}, u32[]{:S(2)}, u32[]{:S(2)}) %all-to-all-start) | async-done | bytes 8388640 | tf_op jit(solution)/shard_map/all_to_all | solution.py:12
  271.2 11.1 %fusion.91 = (f32[1,1024,1024]{2,0,1:T(1,128)}, f32[1,1024,1024]{2,0,1:T(1,128)S(1)}) fusion(f32[2,1024,1024]{2,0,1:T(2,128)} %all-to-all-done), kind=kLoop, calls=%fused_computation.65 | loop fusion | bytes 16777216 | tf_op jit(solution)/shard_map/slice | solution.py:45
  282.3 2.0 copy-done.3
  284.2 5.1 %fusion.36 = f32[1024,256]{0,1:T(8,128)} fusion(f32[1024,256]{0,1:T(8,128)S(1)} %copy.24, f32[1,1024,1024]{2,0,1:T(1,128)S(1)} %get-tuple-element.6, f32[1024,256]{0,1:T(8,128)S(1)} %copy.20, pred[]{:T(512)S(6)} %eq.2), kind=kOutput, calls=%fused_computation.40 | convolution fusion | flops 3221749760 | bytes 7340033 | tf_op jit(solution)/shard_map/dot_general | solution.py:44
  289.3 6.1 %fusion.19 = f32[256,1024]{1,0:T(8,128)S(1)} fusion(f32[1024,256]{0,1:T(8,128)} %fusion.36, f32[2,1024,1024]{2,1,0:T(8,128)} %all-gather.2.cloned.1.call-done), kind=kOutput, calls=%fused_computation.21 | convolution fusion | flops 3221225472 | bytes 6291456 | tf_op jit(solution)/shard_map/dot_general | solution.py:50
  295.4 0.0 copy-start.5
  295.4 7.6 %fusion.60 = f32[1024,256]{0,1:T(8,128)S(1)} fusion(f32[1024,256]{0,1:T(8,128)S(1)} %copy.25, f32[256,1024]{1,0:T(8,128)S(1)} %fusion.19, f32[1,1024,1024]{2,0,1:T(1,128)} %get-tuple-element.5), kind=kOutput, calls=%fused_computation.48 | convolution fusion | flops 3221487616 | bytes 7340032 | tf_op jit(solution)/shard_map/dot_general | solution.py:44
  303.1 0.0 copy-done
  303.1 0.0 copy-start.4
  303.1 3.7 fusion.23
  306.8 0.0 copy-done.5
  306.8 0.0 copy-start.11
  306.9 3.4 collective-permute-start
  310.3 24.0 %collective-permute-done = f32[1024,256]{0,1:T(8,128)S(1)} collective-permute-done((f32[1024,256]{0,1:T(8,128)S(1)}, f32[1024,256]{0,1:T(8,128)S(1)}, u32[]{:S(2)}, u32[]{:S(2)}) %collective-permute-start) | collective-permute-done | bytes 1048608 | tf_op jit(solution)/shard_map/ppermute | solution.py:18
  334.3 0.0 copy-done.11
  334.3 4.2 fusion.42
  338.4 0.0 copy-start.1
  338.5 3.7 fusion.18
  342.2 4.1 fusion.66
  346.3 3.9 fusion.22
  350.3 2.5 collective-permute-start.1
  352.8 24.0 %collective-permute-done.1 = f32[1024,256]{0,1:T(8,128)S(1)} collective-permute-done((f32[1024,256]{0,1:T(8,128)S(1)}, f32[1024,256]{0,1:T(8,128)S(1)}, u32[]{:S(2)}, u32[]{:S(2)}) %collective-permute-start.1) | collective-permute-done | bytes 1048608 | tf_op jit(solution)/shard_map/ppermute | solution.py:18
  376.8 4.2 fusion.48
  381.0 0.0 copy-done.13
  381.0 3.7 fusion.17
  384.8 4.1 fusion.72
  388.9 4.9 %fusion.21 = f32[256,1024]{1,0:T(8,128)} fusion(f32[1024,256]{0,1:T(8,128)S(1)} %fusion.72, f32[2,1024,1024]{2,1,0:T(8,128)S(1)} %copy-done), kind=kOutput, calls=%fused_computation.23 | convolution fusion | flops 3221225472 | bytes 6291456 | tf_op jit(solution)/shard_map/dot_general | solution.py:50
  393.8 0.0 copy-done.9
  393.8 1.9 collective-permute-start.2
  395.7 24.0 %collective-permute-done.2 = f32[1024,256]{0,1:T(8,128)} collective-permute-done((f32[1024,256]{0,1:T(8,128)}, f32[1024,256]{0,1:T(8,128)}, u32[]{:S(2)}, u32[]{:S(2)}) %collective-permute-start.2) | collective-permute-done | bytes 1048608 | tf_op jit(solution)/shard_map/ppermute | solution.py:18
  419.8 7.3 %fusion.54 = f32[1024,256]{0,1:T(8,128)S(1)} fusion(f32[1024,256]{0,1:T(8,128)S(1)} %copy.24, f32[1,1024,1024]{2,0,1:T(1,128)} %copy-done.3, f32[1024,256]{0,1:T(8,128)S(1)} %copy.20, f32[1024,256]{0,1:T(8,128)} %collective-permute-done.2, pred[]{:T(512)S(6)} %eq.2), kind=kOutput, calls=%fused_computation.46 | convolution fusion | flops 3221749760 | bytes 8388609 | tf_op jit(solution)/shard_map/dot_general | solution.py:44
  427.0 0.0 slice-start.1
  427.0 6.1 %fusion.16 = f32[256,1024]{1,0:T(8,128)S(1)} fusion(f32[1024,256]{0,1:T(8,128)S(1)} %fusion.54, f32[2,1024,1024]{2,1,0:T(8,128)} %all-gather.2.cloned.1.call-done), kind=kOutput, calls=%fused_computation.18 | convolution fusion | flops 3221225472 | bytes 6291456 | tf_op jit(solution)/shard_map/dot_general | solution.py:50
  433.2 0.0 copy-done.2
  433.2 4.1 fusion.78
  437.4 3.8 fusion.32
  441.2 2.2 maximum_select_fusion
  443.4 1.8 copy.21
  (25 shorter events, 0.0 us)
Async XLA Ops:
  14.7 5.9 %copy-start.15 = (f32[2048,256]{1,0:T(8,128)S(1)}, f32[2048,256]{1,0:T(8,128)}, u32[]{:S(2)}) copy-start(f32[2048,256]{1,0:T(8,128)} %param.4) | copy-start | bytes 6291460
  14.7 256.4 %all-to-all-start = ((f32[2,1024,1024]{2,0,1:T(2,128)}), f32[2,1024,1024]{2,0,1:T(2,128)}, u32[]{:S(2)}, u32[]{:S(2)}) async-start(f32[2,1024,1024]{2,0,1:T(2,128)} %bitcast.137), calls=%async_computation | async-start | bytes 16777216 | tf_op jit(solution)/shard_map/all_to_all | solution.py:12
  19.9 269.4 %all-gather.2.cloned.1.call-start = ((), (), s32[]{:S(2)}) async-start(), calls=%async_computation.1 | async-start | bytes 9437184 | tf_op jit(solution)/shard_map/all_gather | solution.py:29
  282.3 2.0 copy-start.3
  289.3 13.8 %copy-start = (f32[2,1024,1024]{2,1,0:T(8,128)S(1)}, f32[2,1024,1024]{2,1,0:T(8,128)}, u32[]{:S(2)}) copy-start(f32[2,1024,1024]{2,1,0:T(8,128)} %all-gather.2.cloned.1.call-done) | copy-start | bytes 25165828
  295.4 11.4 %copy-start.5 = (f32[256,1024]{1,0:T(8,128)}, f32[256,1024]{1,0:T(8,128)S(1)}, u32[]{:S(2)}) copy-start(f32[256,1024]{1,0:T(8,128)S(1)} %fusion.19) | copy-start | bytes 3145732
  303.1 31.2 %copy-start.4 = (f32[1,1024,1024]{2,0,1:T(1,128)S(1)}, f32[1,1024,1024]{2,0,1:T(1,128)}, u32[]{:S(2)}) copy-start(f32[1,1024,1024]{2,0,1:T(1,128)} %copy-done.3) | copy-start | bytes 12582916
  306.8 27.4 %copy-start.11 = (f32[256,1024]{1,0:T(8,128)}, f32[256,1024]{1,0:T(8,128)S(1)}, u32[]{:S(2)}) copy-start(f32[256,1024]{1,0:T(8,128)S(1)} %fusion.23) | copy-start | bytes 3145732
  306.9 27.4 %collective-permute-start = (f32[1024,256]{0,1:T(8,128)S(1)}, f32[1024,256]{0,1:T(8,128)S(1)}, u32[]{:S(2)}, u32[]{:S(2)}) collective-permute-start(f32[1024,256]{0,1:T(8,128)S(1)} %bitcast.142), channel_id=1, source_target_pairs={{0,8},{8,16},{16,24},{1,9},{9,17},{17,25},{2,10},{10,18},{18,26},{... | collective-permute-start | bytes 3145736 | tf_op jit(solution)/shard_map/ppermute | solution.py:18
  338.4 3.8 copy-start.1
  342.2 8.0 %copy-start.7 = (f32[256,1024]{1,0:T(8,128)}, f32[256,1024]{1,0:T(8,128)S(1)}, u32[]{:S(2)}) copy-start(f32[256,1024]{1,0:T(8,128)S(1)} %fusion.18) | copy-start | bytes 3145732
  350.3 30.7 %copy-start.13 = (f32[256,1024]{1,0:T(8,128)}, f32[256,1024]{1,0:T(8,128)S(1)}, u32[]{:S(2)}) copy-start(f32[256,1024]{1,0:T(8,128)S(1)} %fusion.22) | copy-start | bytes 3145732
  350.3 26.5 %collective-permute-start.1 = (f32[1024,256]{0,1:T(8,128)S(1)}, f32[1024,256]{0,1:T(8,128)S(1)}, u32[]{:S(2)}, u32[]{:S(2)}) collective-permute-start(f32[1024,256]{0,1:T(8,128)S(1)} %bitcast.144), channel_id=1, source_target_pairs={{0,8},{8,16},{16,24},{1,9},{9,17},{17,25},{2,10},{10,18},{18,26},{... | collective-permute-start | bytes 3145736 | tf_op jit(solution)/shard_map/ppermute | solution.py:18
  384.7 9.0 %copy-start.9 = (f32[256,1024]{1,0:T(8,128)}, f32[256,1024]{1,0:T(8,128)S(1)}, u32[]{:S(2)}) copy-start(f32[256,1024]{1,0:T(8,128)S(1)} %fusion.17) | copy-start | bytes 3145732
  393.8 26.0 %collective-permute-start.2 = (f32[1024,256]{0,1:T(8,128)}, f32[1024,256]{0,1:T(8,128)}, u32[]{:S(2)}, u32[]{:S(2)}) collective-permute-start(f32[1024,256]{0,1:T(8,128)} %bitcast.11), channel_id=1, source_target_pairs={{0,8},{8,16},{16,24},{1,9},{9,17},{17,25},{2,10},{10,18},{18,26},{... | collective-permute-start | bytes 3145736 | tf_op jit(solution)/shard_map/ppermute | solution.py:18
  419.8 13.4 %copy-start.2 = (f32[1,1024,1024]{2,0,1:T(1,128)S(1)}, f32[1,1024,1024]{2,0,1:T(1,128)}, u32[]{:S(2)}) copy-start(f32[1,1024,1024]{2,0,1:T(1,128)} %get-tuple-element.5) | copy-start | bytes 12582916
  419.8 17.6 %slice-start = ((s8[8388608]{0:T(1024)(128)(4,1)}), s8[4194304]{0:T(1024)(128)(4,1)S(1)}, s32[]{:S(2)}) async-start(s8[8388608]{0:T(1024)(128)(4,1)} %bitcast.135), calls=%async_computation.2 | async-start | bytes 8388608
  427.0 10.3 %slice-start.1 = ((s8[8388608]{0:T(1024)(128)(4,1)}), s8[4194304]{0:T(1024)(128)(4,1)S(1)}, s32[]{:S(2)}) async-start(s8[8388608]{0:T(1024)(128)(4,1)} %bitcast.135), calls=%async_computation.3 | async-start | bytes 8388608
  437.4 3.8 copy-start.6
  437.4 3.8 copy-start.8
  437.4 3.8 copy-start.10
  437.4 3.8 copy-start.12
  437.4 3.8 copy-start.14
Sparse Core Ops, SparseCore 0:
  22.3 152.0 all-gather.1
